TPU v7x, 256 devices: a whole 4x4x8 slice. The times are simulated.
256 devices in a mesh: pts: 64 (over x, z, core), rep: 4 (over y).
Axes of the slice: x: 4, y: 4, z: 8, core: 2. Of those that a mesh axis runs over, the one named last changes fastest.
Arguments:
- points: bfloat16 [4, 131072, 512], P('rep', 'pts'), may hold values from -60 to 60
- counts: int32 [4, 64], P('rep', 'pts'), may hold values from 0 to 2048, as said below
- hilbert_rank: int32 [4, 131072], P('rep', 'pts'), may hold values from 0 to 65535, as said below
- patch_shift: int32 [4], P('rep'), may hold values from 1 to 1023
- norm_gain: float32 [512], replicated, may hold values from 0.1 to 1.9
- project_in: bfloat16 [512, 1536], replicated, may hold values from -8 to 8
- project_out: bfloat16 [512, 512], replicated, may hold values from -0.25 to 0.25
- cotangent: bfloat16 [4, 65536, 512], P('rep', 'pts'), may hold values from -6 to 6
Outputs:
- block_out: bfloat16 [4, 65536, 512], P('rep', 'pts')
- grad_points: bfloat16 [4, 131072, 512], P('rep', 'pts')
- grad_project_in: float32 [512, 1536], replicated
- grad_project_out: float32 [512, 512], replicated
- grad_gain: float32 [512], replicated
Inputs may be any that keep to these rules, and one draw needn't show every extreme that they name: The valid points of shard d fill its first counts[b, d] slots; the counts of a scan sum to 65536, and in every scan some shard holds exactly 2048. `hilbert_rank`: the ranks of the valid slots of a scan are a permutation of 0 to 65535. At most 32 valid slots of one shard have ranks in one block [m * 1024, (m + 1) * 1024); in every scan some shard has exactly 32 in every block. Slots beyond the count hold arbitrary ranks.
All inputs are finite; a program needn't handle non-finite values.
Results may differ from a plain program's by a relative error of at most 0.012.
The roundings to bfloat16 on the way count: a program that leaves them out, or rounds other values in their place, can miss the bound.
Values may be sent and summed in bfloat16 or wider, within the bound.
A program may use at most 128 MiB of HBM per device.

v0:
```python
import math
import jax
import jax.numpy as jnp
from jax import lax
from jax.sharding import PartitionSpec as P

HEAD_DIM = 64
PATCH = 1024
EPSILON = 1e-05


def shifted(value, axis, steps):
    count = lax.axis_size(axis)
    pairs = [(source, (source + steps) % count) for source in range(count)]
    return lax.ppermute(value, axis, pairs)


def layer_stats(rows_in):
    values = rows_in.astype(jnp.float32)
    centre = jnp.mean(values, axis=-1, keepdims=True)
    deviation = values - centre
    inverse = lax.rsqrt(jnp.mean(deviation * deviation, axis=-1, keepdims=True) + EPSILON)
    return (deviation * inverse, inverse)


def split_heads(projected):
    row_count = projected.shape[0]
    head_count = projected.shape[1] // (3 * HEAD_DIM)
    shaped = projected.reshape(row_count // PATCH, PATCH, 3, head_count, HEAD_DIM)
    return jnp.transpose(shaped, (2, 3, 0, 1, 4))


def join_heads(per_head):
    head_count, group_count, patch_rows, depth = per_head.shape
    return jnp.transpose(per_head, (1, 2, 0, 3)).reshape(
        group_count * patch_rows, head_count * depth
    )


def head_forward(triple):
    queries, key_rows, value_rows = triple
    logits = jnp.einsum(
        "gqd,gkd->gqk", queries, key_rows, preferred_element_type=jnp.float32
    ) * HEAD_DIM ** (-0.5)
    attention = jax.nn.softmax(logits, axis=-1).astype(jnp.bfloat16)
    return jnp.einsum(
        "gqk,gkd->gqd", attention, value_rows, preferred_element_type=jnp.float32
    ).astype(jnp.bfloat16)


def attend_forward(projected):
    parts = split_heads(projected)
    return join_heads(lax.map(head_forward, (parts[0], parts[1], parts[2])))


def head_backward(quadruple):
    queries, key_rows, value_rows, grad_rows = quadruple
    logits = jnp.einsum(
        "gqd,gkd->gqk", queries, key_rows, preferred_element_type=jnp.float32
    ) * HEAD_DIM ** (-0.5)
    attention_f32 = jax.nn.softmax(logits, axis=-1)
    attention = attention_f32.astype(jnp.bfloat16)
    grad_values = jnp.einsum(
        "gqk,gqd->gkd", attention, grad_rows, preferred_element_type=jnp.float32
    ).astype(jnp.bfloat16)
    grad_attention = jnp.einsum(
        "gqd,gkd->gqk", grad_rows, value_rows, preferred_element_type=jnp.float32
    )
    row_dot = jnp.sum(grad_attention * attention_f32, axis=-1, keepdims=True)
    grad_logits = (attention_f32 * (grad_attention - row_dot) * HEAD_DIM ** (-0.5)).astype(
        jnp.bfloat16
    )
    grad_queries = jnp.einsum(
        "gqk,gkd->gqd", grad_logits, key_rows, preferred_element_type=jnp.float32
    ).astype(jnp.bfloat16)
    grad_keys = jnp.einsum(
        "gqk,gqd->gkd", grad_logits, queries, preferred_element_type=jnp.float32
    ).astype(jnp.bfloat16)
    return jnp.stack([grad_queries, grad_keys, grad_values])


def attend_backward(projected, grad_mixed):
    parts = split_heads(projected)
    row_count = projected.shape[0]
    head_count = parts.shape[1]
    grad_parts = jnp.transpose(
        grad_mixed.reshape(row_count // PATCH, PATCH, head_count, HEAD_DIM), (2, 0, 1, 3)
    )
    stacked = lax.map(head_backward, (parts[0], parts[1], parts[2], grad_parts))
    return jnp.transpose(stacked, (2, 3, 1, 0, 4)).reshape(row_count, 3 * head_count * HEAD_DIM)


def route_slots(rank_row, point_count, total, row_count, shard_count, send_size):
    slot_total = rank_row.shape[0]
    live_slot = jnp.arange(slot_total, dtype=jnp.int32) < point_count
    moved = rank_row % total
    target_shard = jnp.where(live_slot, moved // row_count, shard_count)
    matches = (target_shard[:, None] == jnp.arange(shard_count, dtype=jnp.int32)[None, :]).astype(
        jnp.int32
    )
    ordinal = jnp.sum((jnp.cumsum(matches, axis=0) - 1) * matches, axis=1)
    target = jnp.where(live_slot, target_shard * send_size + ordinal, shard_count * send_size)
    return (live_slot, target, moved % row_count)


def on_device(
    points, counts, hilbert_rank, patch_shift, norm_gain, project_in, project_out, cotangent
):
    shard_count = lax.axis_size("pts")
    row_count = cotangent.shape[1]
    width = points.shape[2]
    slot_size = points.shape[1] // shard_count
    total = row_count * shard_count
    offset = patch_shift[0]
    live_slot, target, position = route_slots(
        hilbert_rank[0], counts[0, 0], total, row_count, shard_count, slot_size
    )
    outgoing = (
        jnp.zeros((shard_count * slot_size, width), jnp.bfloat16)
        .at[target]
        .set(points[0], mode="drop")
    )
    out_position = (
        jnp.full((shard_count * slot_size,), -1, jnp.int32).at[target].set(position, mode="drop")
    )
    incoming, in_position = (
        lax.all_to_all(outgoing, "pts", split_axis=0, concat_axis=0, tiled=True),
        lax.all_to_all(out_position, "pts", split_axis=0, concat_axis=0, tiled=True),
    )
    placed = jnp.where(in_position < 0, row_count, in_position)
    ordered = jnp.zeros((row_count, width), jnp.bfloat16).at[placed].set(incoming, mode="drop")
    unit_rows, inverse = layer_stats(ordered)
    normed = (unit_rows * norm_gain).astype(jnp.bfloat16)
    projected = jnp.dot(normed, project_in, preferred_element_type=jnp.float32).astype(jnp.bfloat16)
    cot_rows = cotangent[0]
    next_rows = shifted(projected, "pts", -1)
    window_in = lax.dynamic_slice_in_dim(
        jnp.concatenate([projected, next_rows], axis=0), offset, row_count, 0
    )
    window_mixed = attend_forward(window_in)
    tail_rows = shifted(window_mixed, "pts", 1)
    mixed_rows = lax.dynamic_slice_in_dim(
        jnp.concatenate([tail_rows, window_mixed], axis=0), PATCH - offset, row_count, 0
    )
    block_rows = (
        ordered.astype(jnp.float32)
        + jnp.dot(mixed_rows, project_out, preferred_element_type=jnp.float32)
    ).astype(jnp.bfloat16)
    grad_mixed = jnp.dot(cot_rows, project_out.T, preferred_element_type=jnp.float32).astype(
        jnp.bfloat16
    )
    grad_out = jnp.dot(mixed_rows.T, cot_rows, preferred_element_type=jnp.float32)
    next_grads = shifted(grad_mixed, "pts", -1)
    window_grad = lax.dynamic_slice_in_dim(
        jnp.concatenate([grad_mixed, next_grads], axis=0), offset, row_count, 0
    )
    grad_window = attend_backward(window_in, window_grad)
    spread = lax.dynamic_update_slice(
        jnp.zeros((row_count + PATCH, 3 * width), jnp.bfloat16), grad_window, (offset, jnp.int32(0))
    )
    returned = shifted(spread[row_count:], "pts", 1)
    grad_projected = spread[:row_count].at[:PATCH].add(returned)
    grad_in = jnp.dot(normed.T, grad_projected, preferred_element_type=jnp.float32)
    grad_normed = jnp.dot(grad_projected, project_in.T, preferred_element_type=jnp.float32)
    grad_scale = jnp.sum(grad_normed * unit_rows, axis=0)
    weighted = grad_normed * norm_gain
    branch = inverse * (
        weighted
        - jnp.mean(weighted, axis=-1, keepdims=True)
        - unit_rows * jnp.mean(weighted * unit_rows, axis=-1, keepdims=True)
    )
    grad_ordered = (cot_rows.astype(jnp.float32) + branch).astype(jnp.bfloat16)
    safe_position = jnp.clip(in_position, 0, row_count - 1)
    returning = jnp.where(
        in_position[:, None] >= 0, grad_ordered[safe_position], jnp.zeros((), jnp.bfloat16)
    )
    arrived = lax.all_to_all(returning, "pts", split_axis=0, concat_axis=0, tiled=True)
    safe_target = jnp.clip(target, 0, shard_count * slot_size - 1)
    grad_points = jnp.where(live_slot[:, None], arrived[safe_target], jnp.zeros((), jnp.bfloat16))
    summed_in, summed_out, summed_scale = lax.psum((grad_in, grad_out, grad_scale), ("pts", "rep"))
    factor = 1.0 / math.sqrt(total * lax.axis_size("rep"))
    return (
        block_rows[None],
        grad_points[None],
        summed_in * factor,
        summed_out * factor,
        summed_scale * factor,
    )


def solution(mesh):
    return jax.shard_map(
        on_device,
        mesh=mesh,
        in_specs=(
            P("rep", "pts", None),
            P("rep", "pts"),
            P("rep", "pts"),
            P("rep"),
            P(),
            P(),
            P(),
            P("rep", "pts", None),
        ),
        out_specs=(P("rep", "pts", None), P("rep", "pts", None), P(), P(), P()),
        check_vma=False,
    )
```

profile of v0, /device:TPU:97, one launch (start us, length us, event | category | flops | bytes accessed | tf_op | source)
XLA Modules:
  0.0 731.6 jit_solution(16514262569084634420)
XLA Ops:
  8.8 18.1 %reduce-window.6 = s32[64,16,128]{2,1,0:T(8,128)S(1)} reduce-window(s32[64,16,128]{2,1,0:T(8,128)S(1)} %fusion.81, s32[]{:T(128)} %constant.143.clone.1), window={size=1x1x128 pad=0_0x0_0x127_0}, to_apply=%region_0.1 | reduce-window | flops 16646144 | bytes 1048580 | tf_op jit(solution)/shard_map/reduce-window
  28.9 8.0 %scatter_custom_fusion = s32[2048]{0:T(1024)S(1)} fusion(s32[2048]{0:T(1024)S(1)} %bitcast.195, s32[2048]{0:T(1024)S(1)} %get-tuple-element.159, s32[]{:T(128)} %constant.142.clone.1), kind=kCustom, calls=%fused_computation.164 | custom fusion | bytes 8196 | tf_op jit(solution)/shard_map/scatter | solution.py:124
  37.6 11.0 %all-to-all-start = ((s32[64,32,1]{1,2,0:T(1,128)}), s32[64,32,1]{1,2,0:T(1,128)S(1)}, u32[]{:S(2)}, u32[]{:S(2)}) async-start(s32[64,32,1]{1,2,0:T(1,128)} %bitcast.21), calls=%async_computation | async-start | bytes 65536 | tf_op jit(solution)/shard_map/all_to_all | solution.py:128
  48.6 11.0 %scatter_custom_fusion.1 = bf16[2048,512]{1,0:T(8,128)(2,1)} fusion(s32[2048]{0:T(1024)S(1)} %bitcast.196, bf16[1,2048,512]{2,1,0:T(8,128)(2,1)S(1)} %copy-done, bf16[]{:T(256)} %constant.141.clone.1), kind=kCustom, calls=%fused_computation.88 | custom fusion | bytes 4194306 | tf_op jit(solution)/shard_map/scatter | solution.py:121
  59.6 10.3 %all-to-all-start.1 = ((bf16[64,32,512]{2,1,0:T(8,128)(2,1)}), bf16[64,32,512]{2,1,0:T(8,128)(2,1)S(1)}, u32[]{:S(2)}, u32[]{:S(2)}) async-start(bf16[64,32,512]{2,1,0:T(8,128)(2,1)} %bitcast.182), calls=%async_computation.1 | async-start | bytes 4194304 | tf_op jit(solution)/shard_map/all_to_all | solution.py:127
  71.3 47.5 %all-to-all-done.1 = bf16[64,32,512]{2,1,0:T(8,128)(2,1)S(1)} async-done(((bf16[64,32,512]{2,1,0:T(8,128)(2,1)}), bf16[64,32,512]{2,1,0:T(8,128)(2,1)S(1)}, u32[]{:S(2)}, u32[]{:S(2)}) %all-to-all-start.1) | async-done | bytes 2097184 | tf_op jit(solution)/shard_map/all_to_all | solution.py:127
  118.8 22.3 %scatter_custom_fusion.2 = bf16[1024,512]{1,0:T(8,128)(2,1)S(1)} fusion(s32[2048]{0:T(1024)S(1)} %bitcast.194, bf16[2048,512]{1,0:T(8,128)(2,1)S(1)} %bitcast.184, bf16[]{:T(256)} %constant.141.clone.1), kind=kCustom, calls=%fused_computation.113 | custom fusion | bytes 1048578 | tf_op jit(solution)/shard_map/scatter | solution.py:131
  142.5 3.5 convolution_convert_fusion.2
  149.2 46.3 %collective-permute-done.2 = bf16[1024,512]{1,0:T(8,128)(2,1)} collective-permute-done((bf16[1024,512]{1,0:T(8,128)(2,1)S(1)}, bf16[1024,512]{1,0:T(8,128)(2,1)}, u32[]{:S(2)}, u32[]{:S(2)}) %collective-permute-start.2) | collective-permute-done | bytes 1048608 | tf_op jit(solution)/shard_map/ppermute | solution.py:15
  195.5 2.6 fusion.69
  199.5 6.7 fusion.50
  206.2 4.6 copy.47
  210.9 3.7 slice_bitcast_fusion
  214.5 1.8 copy.50
  216.3 2.0 copy.49
  218.3 2.7 copy.48
  221.0 85.2 %while.23 = (s32[]{:T(128)}, bf16[8,3,1,1024,64]{3,4,0,1,2:T(8,128)(2,1)}, bf16[8,1,1024,64]{3,2,1,0:T(8,128)(2,1)}, bf16[8,1,1024,64]{3,2,1,0:T(8,128)(2,1)S(1)...) while((s32[]{:T(128)}, bf16[8,3,1,1024,64]{3,4,0,1,2:T(8,128)(2,1)}, ...), condition=%wide.region_16.17_spmd, body=%wide.region_12.16_spmd.sunk | while | flops 694481920 | bytes 38451300 | solution.py:89
  223.4 1.9 fusion.129
  225.3 2.0 multiply_reduce_fusion.9
  234.1 1.9 fusion.129
  236.0 2.0 multiply_reduce_fusion.9
  239.8 1.7 fusion.130
  244.7 1.9 fusion.129
  246.6 2.0 multiply_reduce_fusion.9
  250.5 1.7 fusion.130
  255.4 1.9 fusion.129
  257.3 2.0 multiply_reduce_fusion.9
  261.1 1.7 fusion.130
  266.0 1.9 fusion.129
  267.9 2.0 multiply_reduce_fusion.9
  271.8 1.7 fusion.130
  276.7 1.9 fusion.129
  278.5 2.0 multiply_reduce_fusion.9
  287.3 1.9 fusion.129
  289.2 2.0 multiply_reduce_fusion.9
  293.0 1.7 fusion.130
  297.9 1.9 fusion.129
  299.8 2.0 multiply_reduce_fusion.9
  303.7 1.7 fusion.130
  306.2 3.5 broadcast_in_dim.94
  309.6 31.6 %dynamic_update_slice.11 = bf16[2048,1536]{0,1:T(8,128)(2,1)} dynamic-update-slice(bf16[2048,1536]{0,1:T(8,128)(2,1)} %broadcast_in_dim.94, bf16[1024,1536]{0,1:T(8,128)(2,1)} %bitcast.183, s32[]{:T(128)S(6)} %select_n.180, s32[]{:T(128)} %constant.143.clone.1) | dynamic-update-slice | bytes 6291460 | tf_op jit(solution)/shard_map/dynamic_update_slice | solution.py:158
  341.3 3.9 slice.55
  345.1 40.1 %while.22 = (s32[]{:T(128)}, bf16[8,1,1024,64]{2,3,1,0:T(8,128)(2,1)}, bf16[8,1,1024,64]{3,2,1,0:T(8,128)(2,1)}, bf16[8,1,1024,64]{3,2,1,0:T(8,128)(2,1)S(1)}, bf16[8,1,1024,64]{3,2,1,0:T(8,128)(2,1)}, /*index=5*/s32[]{:T(128)}) while((s32[]{:T(128)}, bf16[8,1,1024,64]{2,3,1,0:T(8,128)(2,1)}, bf16[8,1,1024,64]{3,2,1,0:T(8,128)(2,1)}, ...), condition=%wide.region_11.12_spmd, body=%wide.region_8.11_spmd.sunk | while | flops 277936128 | bytes 13523021 | solution.py:53
  347.5 2.6 fusion.121
  352.5 2.6 fusion.121
  357.6 2.6 fusion.121
  362.6 2.6 fusion.121
  367.6 2.6 fusion.121
  372.6 2.6 fusion.121
  377.6 2.6 fusion.121
  382.6 2.6 fusion.121
  386.1 5.2 fusion.63
  392.4 9.2 %gather_fusion = bf16[2048,512]{1,0:T(8,128)(2,1)} fusion(bf16[1024,512]{1,0:T(8,128)(2,1)S(1)} %fusion.62, s32[2048]{0:T(1024)S(1)} %copy-done.6), kind=kCustom, calls=%fused_computation | custom fusion | bytes 4202496 | tf_op jit(solution)/shard_map/gather | solution.py:175
  401.6 2.7 broadcast_select_fusion
  404.3 8.9 %all-to-all-start.2 = ((bf16[64,32,512]{2,1,0:T(8,128)(2,1)}), bf16[64,32,512]{2,1,0:T(8,128)(2,1)}, u32[]{:S(2)}, u32[]{:S(2)}) async-start(bf16[64,32,512]{2,1,0:T(8,128)(2,1)} %broadcast_select_fusion), calls=%async_computation.2 | async-start | bytes 4194304 | tf_op jit(solution)/shard_map/all_to_all | solution.py:177
  413.3 3.3 fusion.71
  416.6 6.7 fusion.75
  424.6 3.7 fusion.68
  428.4 81.7 %psum.23 = f32[512]{0:T(512)S(1)} all-reduce(f32[512]{0:T(512)S(1)} %get-tuple-element.119), channel_id=1, replica_groups=mesh['pts'=64,'rep'=4] {'pts','rep'}, use_global_device_ids=true, to_apply=%region_22.23 | all-reduce | flops 512 | bytes 4096 | tf_op jit(solution)/shard_map/psum | solution.py:180
  510.6 193.6 %all-reduce.3.cloned.1.call-done = (f32[512,1536]{1,0:T(8,128)}, f32[512,512]{1,0:T(8,128)}) async-done(((f32[512,1536]{1,0:T(8,128)}, f32[512,512]{1,0:T(8,128)}), (f32[512,1536]{1,0:T(8,128)}, f32[512,512]{1,0:T(8,128)})) %all-reduce.3.cloned.1.call-update) | async-done | bytes 4194320 | tf_op jit(solution)/shard_map/psum | solution.py:180
  704.2 2.3 broadcast_multiply_fusion.1
  706.5 3.8 broadcast_multiply_fusion
  710.3 11.3 %gather_fusion.1 = bf16[2048,512]{1,0:T(8,128)(2,1)} fusion(bf16[2048,512]{1,0:T(8,128)(2,1)} %bitcast.44, s32[2048]{0:T(1024)S(1)} %broadcast_clamp_fusion), kind=kCustom, calls=%fused_computation.1 | custom fusion | bytes 4202496 | tf_op jit(solution)/shard_map/gather | solution.py:179
  721.6 2.7 bitcast_select_fusion
  (129 shorter events, 76.3 us)
Async XLA Ops:
  7.2 41.4 %copy-start = (bf16[1,2048,512]{2,1,0:T(8,128)(2,1)S(1)}, bf16[1,2048,512]{2,1,0:T(8,128)(2,1)}, u32[]{:S(2)}) copy-start(bf16[1,2048,512]{2,1,0:T(8,128)(2,1)} %param.16) | copy-start | bytes 6291460
  8.7 19.2 %copy-start.4 = (s32[1,2048]{1,0:T(1,128)S(1)}, s32[1,2048]{1,0:T(1,128)}, u32[]{:S(2)}) copy-start(s32[1,2048]{1,0:T(1,128)} %param.18) | copy-start | bytes 24580
  37.6 22.0 %all-to-all-start = ((s32[64,32,1]{1,2,0:T(1,128)}), s32[64,32,1]{1,2,0:T(1,128)S(1)}, u32[]{:S(2)}, u32[]{:S(2)}) async-start(s32[64,32,1]{1,2,0:T(1,128)} %bitcast.21), calls=%async_computation | async-start | bytes 65536 | tf_op jit(solution)/shard_map/all_to_all | solution.py:128
  59.6 59.2 %all-to-all-start.1 = ((bf16[64,32,512]{2,1,0:T(8,128)(2,1)}), bf16[64,32,512]{2,1,0:T(8,128)(2,1)S(1)}, u32[]{:S(2)}, u32[]{:S(2)}) async-start(bf16[64,32,512]{2,1,0:T(8,128)(2,1)} %bitcast.182), calls=%async_computation.1 | async-start | bytes 4194304 | tf_op jit(solution)/shard_map/all_to_all | solution.py:127
  69.9 72.0 %copy-start.8 = (f32[512]{0:T(512)S(1)}, f32[512]{0:T(512)}, u32[]{:S(2)}) copy-start(f32[512]{0:T(512)} %param.20) | copy-start | bytes 6148
  141.1 1.4 copy-start.9
  142.5 3.6 copy-start.2
  142.5 3.6 copy-start.12
  146.1 53.4 %collective-permute-start = (bf16[1024,1536]{1,0:T(8,128)(2,1)}, bf16[1024,1536]{1,0:T(8,128)(2,1)}, u32[]{:S(2)}, u32[]{:S(2)}) collective-permute-start(bf16[1024,1536]{1,0:T(8,128)(2,1)} %convolution_convert_fusion.2), channel_id=1, source_target_pairs={{0,252},{4,0},{8,4},{12,8},{16,12},{20,16},{24,20},{28,24},{32,28}... | collective-permute-start | bytes 9437192 | tf_op jit(solution)/shard_map/ppermute | solution.py:15
  146.8 48.7 %collective-permute-start.2 = (bf16[1024,512]{1,0:T(8,128)(2,1)S(1)}, bf16[1024,512]{1,0:T(8,128)(2,1)}, u32[]{:S(2)}, u32[]{:S(2)}) collective-permute-start(bf16[1024,512]{1,0:T(8,128)(2,1)S(1)} %convolution_convert_fusion.3), channel_id=1, source_target_pairs={{0,252},{4,0},{8,4},{12,8},{16,12},{20,16},{24,20},{28,24},{32,28}... | collective-permute-start | bytes 3145736 | tf_op jit(solution)/shard_map/ppermute | solution.py:15
  345.1 41.0 %collective-permute-start.3 = (bf16[1024,1536]{0,1:T(8,128)(2,1)}, bf16[1024,1536]{0,1:T(8,128)(2,1)}, u32[]{:S(2)}, u32[]{:S(2)}) collective-permute-start(bf16[1024,1536]{0,1:T(8,128)(2,1)} %slice.55), channel_id=1, source_target_pairs={{0,4},{4,8},{8,12},{12,16},{16,20},{20,24},{24,28},{28,32},{32,36}... | collective-permute-start | bytes 9437192 | tf_op jit(solution)/shard_map/ppermute | solution.py:15
  385.2 6.1 copy-start.3
  385.2 28.1 %collective-permute-start.1 = (bf16[1024,512]{0,1:T(8,128)(2,1)}, bf16[1024,512]{0,1:T(8,128)(2,1)}, u32[]{:S(2)}, u32[]{:S(2)}) collective-permute-start(bf16[1024,512]{0,1:T(8,128)(2,1)} %bitcast.197), channel_id=1, source_target_pairs={{0,4},{4,8},{8,12},{12,16},{16,20},{20,24},{24,28},{28,32},{32,36}... | collective-permute-start | bytes 3145736 | tf_op jit(solution)/shard_map/ppermute | solution.py:15
  391.3 1.0 copy-start.6
  392.4 9.2 %copy-start.5 = (pred[64,32]{1,0:T(8,128)(4,1)S(1)}, pred[64,32]{1,0:T(8,128)(4,1)}, u32[]{:S(2)}) copy-start(pred[64,32]{1,0:T(8,128)(4,1)} %copy.52) | copy-start | bytes 6148
  404.3 9.0 %copy-start.10 = (bf16[8,1,1024,64]{2,3,1,0:T(8,128)(2,1)S(1)}, bf16[8,1,1024,64]{2,3,1,0:T(8,128)(2,1)}, u32[]{:S(2)}) copy-start(bf16[8,1,1024,64]{2,3,1,0:T(8,128)(2,1)} %get-tuple-element.84) | copy-start | bytes 3145732
  404.3 306.0 %all-to-all-start.2 = ((bf16[64,32,512]{2,1,0:T(8,128)(2,1)}), bf16[64,32,512]{2,1,0:T(8,128)(2,1)}, u32[]{:S(2)}, u32[]{:S(2)}) async-start(bf16[64,32,512]{2,1,0:T(8,128)(2,1)} %broadcast_select_fusion), calls=%async_computation.2 | async-start | bytes 4194304 | tf_op jit(solution)/shard_map/all_to_all | solution.py:177
  413.2 291.0 %all-reduce.3.cloned.1.call-start = ((), (), s32[]{:S(2)}) async-start(), calls=%async_computation.3 | async-start | bytes 8388608 | tf_op jit(solution)/shard_map/psum | solution.py:180
  423.3 0.7 copy-start.7
  423.3 1.2 copy-start.11
  423.3 1.4 copy-start.13
  710.3 14.0 %copy-start.1 = (bf16[1,2048,512]{2,1,0:T(8,128)(2,1)S(1)}, bf16[1,2048,512]{2,1,0:T(8,128)(2,1)}, u32[]{:S(2)}) copy-start(bf16[1,2048,512]{2,1,0:T(8,128)(2,1)} %param.16) | copy-start | bytes 6291460
Sparse Core Ops, SparseCore 0:
  423.4 280.7 all-reduce.2
where the time goes:
time: 742 us; the launch traced here: 732 us
  waiting for transfers between devices  287 us (39%)
  local copies, waits for them, and re-layouts  122 us (16%)
  matrix products  120 us (16%)
  blocking collectives  81.7 us (11%)
  other arithmetic  72.8 us (10%)
  starting transfers between devices  31.5 us (4%)
  between operations  16.2 us (2%)
    psum x1, waiting for transfers between devices, on_device(): lax.psum((grad_in, grad_out, grad_scale), ('pts', 'rep'))  194 us
    psum x1, blocking collectives, on_device(): lax.psum((grad_in, grad_out, grad_scale), ('pts', 'rep'))  81.7 us
    all_to_all x1, waiting for transfers between devices, on_device(): lax.all_to_all(outgoing, 'pts', split_axis=0, concat_axis=0, tiled=True)  47.5 us
    ppermute x4, waiting for transfers between devices, shifted(): return lax.ppermute(value, axis, pairs)  46.3 us
    dynamic_update_slice x1, local copies, waits for them, and re-layouts, on_device(): lax.dynamic_update_slice(jnp.zeros((row_count + PATCH, 3 * width), jnp.bf...  31.6 us
    scatter x1, local copies, waits for them, and re-layouts, on_device(): jnp.zeros((row_count, width), jnp.bfloat16).at[placed]  22.3 us
    dot_general x8, matrix products, head_forward(): jnp.einsum('gqk,gkd->gqd', attention, value_rows, preferred_element_type=...  20.9 us
    another operation x2, other arithmetic  18.3 us
  transfers between devices with their start and end apart: 8, of which 3 were waited for; matrix products, arithmetic and copies ran while one was open for 13% of the time, Pallas kernels for 0%

commit v1 on v0

--- a/solution.py
+++ b/solution.py
@@ -177,7 +177,9 @@
     arrived = lax.all_to_all(returning, "pts", split_axis=0, concat_axis=0, tiled=True)
     safe_target = jnp.clip(target, 0, shard_count * slot_size - 1)
     grad_points = jnp.where(live_slot[:, None], arrived[safe_target], jnp.zeros((), jnp.bfloat16))
-    summed_in, summed_out, summed_scale = lax.psum((grad_in, grad_out, grad_scale), ("pts", "rep"))
+    summed_in, summed_out, summed_scale = lax.psum(
+        lax.psum((grad_in, grad_out, grad_scale), "pts"), "rep"
+    )
     factor = 1.0 / math.sqrt(total * lax.axis_size("rep"))
     return (
         block_rows[None],

time: 742 us -> 808 us (1.089)
  the two profiles are of different devices: /device:TPU:97 before, /device:TPU:0 now
where the time goes in v1:
time: 808 us; the launch traced here: 797 us
  waiting for transfers between devices  304 us (38%)
  blocking collectives  138 us (17%)
  matrix products  121 us (15%)
  local copies, waits for them, and re-layouts  118 us (15%)
  other arithmetic  71.2 us (9%)
  starting transfers between devices  28 us (3%)
  between operations  16.1 us (2%)
    psum x1, waiting for transfers between devices, on_device(): lax.psum((grad_in, grad_out, grad_scale), 'pts')  193 us
    psum x1, blocking collectives, on_device(): lax.psum((grad_in, grad_out, grad_scale), 'pts')  128 us
    ppermute x4, waiting for transfers between devices, shifted(): return lax.ppermute(value, axis, pairs)  61.8 us
    all_to_all x1, waiting for transfers between devices, on_device(): lax.all_to_all(outgoing, 'pts', split_axis=0, concat_axis=0, tiled=True)  49.7 us
    dynamic_update_slice x1, local copies, waits for them, and re-layouts, on_device(): lax.dynamic_update_slice(jnp.zeros((row_count + PATCH, 3 * width), jnp.bf...  31.6 us
    scatter x1, local copies, waits for them, and re-layouts, on_device(): jnp.zeros((row_count, width), jnp.bfloat16).at[placed]  22.2 us
    dot_general x8, matrix products, head_forward(): jnp.einsum('gqk,gkd->gqd', attention, value_rows, preferred_element_type=...  20.9 us
    another operation x2, other arithmetic  18.3 us
  transfers between devices with their start and end apart: 9, of which 4 were waited for; matrix products, arithmetic and copies ran while one was open for 12% of the time, Pallas kernels for 0%

profile of v1, /device:TPU:0, one launch (start us, length us, event | category | flops | bytes accessed | tf_op | source)
XLA Modules:
  0.0 797.0 jit_solution(9242106345749315431)
XLA Ops:
  8.8 18.1 %reduce-window.6 = s32[64,16,128]{2,1,0:T(8,128)S(1)} reduce-window(s32[64,16,128]{2,1,0:T(8,128)S(1)} %fusion.81, s32[]{:T(128)} %constant.143.clone.1), window={size=1x1x128 pad=0_0x0_0x127_0}, to_apply=%region_0.1 | reduce-window | flops 16646144 | bytes 1048580 | tf_op jit(solution)/shard_map/reduce-window
  28.9 8.0 %scatter_custom_fusion = s32[2048]{0:T(1024)S(1)} fusion(s32[2048]{0:T(1024)S(1)} %bitcast.196, s32[2048]{0:T(1024)S(1)} %get-tuple-element.161, s32[]{:T(128)} %constant.142.clone.1), kind=kCustom, calls=%fused_computation.164 | custom fusion | bytes 8196 | tf_op jit(solution)/shard_map/scatter | solution.py:124
  37.6 10.2 %all-to-all-start = ((s32[64,32,1]{1,2,0:T(1,128)}), s32[64,32,1]{1,2,0:T(1,128)S(1)}, u32[]{:S(2)}, u32[]{:S(2)}) async-start(s32[64,32,1]{1,2,0:T(1,128)} %bitcast.21), calls=%async_computation | async-start | bytes 65536 | tf_op jit(solution)/shard_map/all_to_all | solution.py:128
  47.9 11.0 %scatter_custom_fusion.1 = bf16[2048,512]{1,0:T(8,128)(2,1)} fusion(s32[2048]{0:T(1024)S(1)} %bitcast.197, bf16[1,2048,512]{2,1,0:T(8,128)(2,1)S(1)} %copy-done, bf16[]{:T(256)} %constant.141.clone.1), kind=kCustom, calls=%fused_computation.88 | custom fusion | bytes 4194306 | tf_op jit(solution)/shard_map/scatter | solution.py:121
  58.9 10.3 %all-to-all-start.1 = ((bf16[64,32,512]{2,1,0:T(8,128)(2,1)}), bf16[64,32,512]{2,1,0:T(8,128)(2,1)S(1)}, u32[]{:S(2)}, u32[]{:S(2)}) async-start(bf16[64,32,512]{2,1,0:T(8,128)(2,1)} %bitcast.183), calls=%async_computation.1 | async-start | bytes 4194304 | tf_op jit(solution)/shard_map/all_to_all | solution.py:127
  70.6 49.7 %all-to-all-done.1 = bf16[64,32,512]{2,1,0:T(8,128)(2,1)S(1)} async-done(((bf16[64,32,512]{2,1,0:T(8,128)(2,1)}), bf16[64,32,512]{2,1,0:T(8,128)(2,1)S(1)}, u32[]{:S(2)}, u32[]{:S(2)}) %all-to-all-start.1) | async-done | bytes 2097184 | tf_op jit(solution)/shard_map/all_to_all | solution.py:127
  120.3 22.2 %scatter_custom_fusion.2 = bf16[1024,512]{1,0:T(8,128)(2,1)S(1)} fusion(s32[2048]{0:T(1024)S(1)} %bitcast.195, bf16[2048,512]{1,0:T(8,128)(2,1)S(1)} %bitcast.185, bf16[]{:T(256)} %constant.141.clone.1), kind=kCustom, calls=%fused_computation.113 | custom fusion | bytes 1048578 | tf_op jit(solution)/shard_map/scatter | solution.py:131
  144.0 3.5 convolution_convert_fusion.2
  150.2 44.3 %collective-permute-done.2 = bf16[1024,512]{1,0:T(8,128)(2,1)} collective-permute-done((bf16[1024,512]{1,0:T(8,128)(2,1)S(1)}, bf16[1024,512]{1,0:T(8,128)(2,1)}, u32[]{:S(2)}, u32[]{:S(2)}) %collective-permute-start.2) | collective-permute-done | bytes 1048608 | tf_op jit(solution)/shard_map/ppermute | solution.py:15
  194.5 2.6 fusion.69
  198.5 6.7 fusion.50
  205.2 4.6 copy.47
  209.8 3.7 slice_bitcast_fusion
  213.5 1.8 copy.50
  215.2 2.0 copy.49
  217.3 2.7 copy.48
  220.0 85.2 %while.23 = (s32[]{:T(128)}, bf16[8,3,1,1024,64]{3,4,0,1,2:T(8,128)(2,1)}, bf16[8,1,1024,64]{3,2,1,0:T(8,128)(2,1)}, bf16[8,1,1024,64]{3,2,1,0:T(8,128)(2,1)S(1)...) while((s32[]{:T(128)}, bf16[8,3,1,1024,64]{3,4,0,1,2:T(8,128)(2,1)}, ...), condition=%wide.region_16.17_spmd, body=%wide.region_12.16_spmd.sunk | while | flops 694481920 | bytes 38451300 | solution.py:89
  222.4 1.9 fusion.129
  224.3 2.0 multiply_reduce_fusion.9
  233.0 1.9 fusion.129
  234.9 2.0 multiply_reduce_fusion.9
  238.8 1.7 fusion.130
  243.7 1.9 fusion.129
  245.6 2.0 multiply_reduce_fusion.9
  254.3 1.9 fusion.129
  256.2 2.0 multiply_reduce_fusion.9
  260.1 1.7 fusion.130
  265.0 1.9 fusion.129
  266.8 2.0 multiply_reduce_fusion.9
  275.6 1.9 fusion.129
  277.5 2.0 multiply_reduce_fusion.9
  281.4 1.7 fusion.130
  286.3 1.9 fusion.129
  288.1 2.0 multiply_reduce_fusion.9
  292.0 1.7 fusion.130
  296.9 1.9 fusion.129
  298.8 2.0 multiply_reduce_fusion.9
  302.6 1.7 fusion.130
  305.1 3.5 broadcast_in_dim.94
  308.6 31.6 %dynamic_update_slice.11 = bf16[2048,1536]{0,1:T(8,128)(2,1)} dynamic-update-slice(bf16[2048,1536]{0,1:T(8,128)(2,1)} %broadcast_in_dim.94, bf16[1024,1536]{0,1:T(8,128)(2,1)} %bitcast.184, s32[]{:T(128)S(6)} %select_n.180, s32[]{:T(128)} %constant.143.clone.1) | dynamic-update-slice | bytes 6291460 | tf_op jit(solution)/shard_map/dynamic_update_slice | solution.py:158
  340.2 3.9 slice.55
  345.5 40.1 %while.22 = (s32[]{:T(128)}, bf16[8,1,1024,64]{2,3,1,0:T(8,128)(2,1)}, bf16[8,1,1024,64]{3,2,1,0:T(8,128)(2,1)}, bf16[8,1,1024,64]{3,2,1,0:T(8,128)(2,1)S(1)}, bf16[8,1,1024,64]{3,2,1,0:T(8,128)(2,1)}, /*index=5*/s32[]{:T(128)}) while((s32[]{:T(128)}, bf16[8,1,1024,64]{2,3,1,0:T(8,128)(2,1)}, bf16[8,1,1024,64]{3,2,1,0:T(8,128)(2,1)}, ...), condition=%wide.region_11.12_spmd, body=%wide.region_8.11_spmd.sunk | while | flops 277936128 | bytes 13523021 | solution.py:53
  347.9 2.6 fusion.121
  352.9 2.6 fusion.121
  357.9 2.6 fusion.121
  362.9 2.6 fusion.121
  367.9 2.6 fusion.121
  373.0 2.6 fusion.121
  378.0 2.6 fusion.121
  383.0 2.6 fusion.121
  385.8 17.5 %collective-permute-done.1 = bf16[1024,512]{0,1:T(8,128)(2,1)S(1)} collective-permute-done((bf16[1024,512]{0,1:T(8,128)(2,1)}, bf16[1024,512]{0,1:T(8,128)(2,1)S(1)}, u32[]{:S(2)}, u32[]{:S(2)}) %collective-permute-start.1) | collective-permute-done | bytes 1048608 | tf_op jit(solution)/shard_map/ppermute | solution.py:15
  403.3 3.7 fusion.71
  407.0 6.7 fusion.75
  413.8 5.3 fusion.63
  420.1 9.2 %gather_fusion = bf16[2048,512]{1,0:T(8,128)(2,1)} fusion(bf16[1024,512]{1,0:T(8,128)(2,1)S(1)} %fusion.62, s32[2048]{0:T(1024)S(1)} %broadcast_clamp_fusion.1), kind=kCustom, calls=%fused_computation | custom fusion | bytes 4202496 | tf_op jit(solution)/shard_map/gather | solution.py:175
  429.3 2.8 broadcast_select_fusion
  432.1 4.7 all-to-all-start.2
  436.8 192.7 %all-reduce.5.cloned.1.call-done = (f32[512,1536]{1,0:T(8,128)}, f32[512,512]{1,0:T(8,128)}) async-done(((f32[512,1536]{1,0:T(8,128)}, f32[512,512]{1,0:T(8,128)}), (f32[512,1536]{1,0:T(8,128)}, f32[512,512]{1,0:T(8,128)})) %all-reduce.5.cloned.1.call-update) | async-done | bytes 4194320 | tf_op jit(solution)/shard_map/psum | solution.py:181
  630.2 4.0 fusion.68
  634.2 127.5 %psum.46 = f32[512]{0:T(512)S(1)} all-reduce(f32[512]{0:T(512)S(1)} %get-tuple-element.119), channel_id=1, replica_groups=mesh['pts'=64,'rep'=4] {'pts'}, use_global_device_ids=true, to_apply=%region_24.25 | all-reduce | flops 512 | bytes 4096 | tf_op jit(solution)/shard_map/psum | solution.py:181
  761.7 10.5 %psum.47 = f32[512]{0:T(512)S(1)} all-reduce(f32[512]{0:T(512)S(1)} %psum.46), channel_id=1, replica_groups=mesh['pts'=64,'rep'=4] {'rep'}, use_global_device_ids=true, to_apply=%region_25.26 | all-reduce | flops 512 | bytes 4096 | tf_op jit(solution)/shard_map/psum | solution.py:180
  772.7 9.2 %gather_fusion.1 = bf16[2048,512]{1,0:T(8,128)(2,1)} fusion(bf16[2048,512]{1,0:T(8,128)(2,1)S(1)} %bitcast.180, s32[2048]{0:T(1024)S(1)} %broadcast_clamp_fusion), kind=kCustom, calls=%fused_computation.1 | custom fusion | bytes 4202496 | tf_op jit(solution)/shard_map/gather | solution.py:179
  781.9 2.7 bitcast_select_fusion
  784.7 4.0 broadcast_multiply_fusion
  (127 shorter events, 78.7 us)
Async XLA Ops:
  7.2 40.7 %copy-start = (bf16[1,2048,512]{2,1,0:T(8,128)(2,1)S(1)}, bf16[1,2048,512]{2,1,0:T(8,128)(2,1)}, u32[]{:S(2)}) copy-start(bf16[1,2048,512]{2,1,0:T(8,128)(2,1)} %param.16) | copy-start | bytes 6291460
  8.7 19.2 %copy-start.5 = (s32[1,2048]{1,0:T(1,128)S(1)}, s32[1,2048]{1,0:T(1,128)}, u32[]{:S(2)}) copy-start(s32[1,2048]{1,0:T(1,128)} %param.18) | copy-start | bytes 24580
  37.6 21.2 %all-to-all-start = ((s32[64,32,1]{1,2,0:T(1,128)}), s32[64,32,1]{1,2,0:T(1,128)S(1)}, u32[]{:S(2)}, u32[]{:S(2)}) async-start(s32[64,32,1]{1,2,0:T(1,128)} %bitcast.21), calls=%async_computation | async-start | bytes 65536 | tf_op jit(solution)/shard_map/all_to_all | solution.py:128
  58.9 61.5 %all-to-all-start.1 = ((bf16[64,32,512]{2,1,0:T(8,128)(2,1)}), bf16[64,32,512]{2,1,0:T(8,128)(2,1)S(1)}, u32[]{:S(2)}, u32[]{:S(2)}) async-start(bf16[64,32,512]{2,1,0:T(8,128)(2,1)} %bitcast.183), calls=%async_computation.1 | async-start | bytes 4194304 | tf_op jit(solution)/shard_map/all_to_all | solution.py:127
  69.2 74.2 %copy-start.7 = (f32[512]{0:T(512)S(1)}, f32[512]{0:T(512)}, u32[]{:S(2)}) copy-start(f32[512]{0:T(512)} %param.20) | copy-start | bytes 6148
  69.2 560.3 %all-reduce.5.cloned.1.call-start = ((), (), s32[]{:S(2)}) async-start(), calls=%async_computation.3 | async-start | bytes 8388608 | tf_op jit(solution)/shard_map/psum | solution.py:181
  142.6 1.4 copy-start.8
  144.0 4.2 copy-start.2
  144.0 4.2 copy-start.10
  147.5 50.9 %collective-permute-start = (bf16[1024,1536]{1,0:T(8,128)(2,1)}, bf16[1024,1536]{1,0:T(8,128)(2,1)}, u32[]{:S(2)}, u32[]{:S(2)}) collective-permute-start(bf16[1024,1536]{1,0:T(8,128)(2,1)} %convolution_convert_fusion.2), channel_id=1, source_target_pairs={{0,252},{4,0},{8,4},{12,8},{16,12},{20,16},{24,20},{28,24},{32,28}... | collective-permute-start | bytes 9437192 | tf_op jit(solution)/shard_map/ppermute | solution.py:15
  149.0 45.5 %collective-permute-start.2 = (bf16[1024,512]{1,0:T(8,128)(2,1)S(1)}, bf16[1024,512]{1,0:T(8,128)(2,1)}, u32[]{:S(2)}, u32[]{:S(2)}) collective-permute-start(bf16[1024,512]{1,0:T(8,128)(2,1)S(1)} %convolution_convert_fusion.3), channel_id=1, source_target_pairs={{0,252},{4,0},{8,4},{12,8},{16,12},{20,16},{24,20},{28,24},{32,28}... | collective-permute-start | bytes 3145736 | tf_op jit(solution)/shard_map/ppermute | solution.py:15
  344.1 63.0 %collective-permute-start.3 = (bf16[1024,1536]{0,1:T(8,128)(2,1)}, bf16[1024,1536]{0,1:T(8,128)(2,1)}, u32[]{:S(2)}, u32[]{:S(2)}) collective-permute-start(bf16[1024,1536]{0,1:T(8,128)(2,1)} %slice.55), channel_id=1, source_target_pairs={{0,4},{4,8},{8,12},{12,16},{16,20},{20,24},{24,28},{28,32},{32,36}... | collective-permute-start | bytes 9437192 | tf_op jit(solution)/shard_map/ppermute | solution.py:15
  385.6 17.8 %collective-permute-start.1 = (bf16[1024,512]{0,1:T(8,128)(2,1)}, bf16[1024,512]{0,1:T(8,128)(2,1)S(1)}, u32[]{:S(2)}, u32[]{:S(2)}) collective-permute-start(bf16[1024,512]{0,1:T(8,128)(2,1)} %bitcast.198), channel_id=1, source_target_pairs={{0,4},{4,8},{8,12},{12,16},{16,20},{20,24},{24,28},{28,32},{32,36}... | collective-permute-start | bytes 3145736 | tf_op jit(solution)/shard_map/ppermute | solution.py:15
  403.3 3.7 copy-start.9
  413.8 5.3 copy-start.3
  432.1 340.7 %all-to-all-start.2 = ((bf16[64,32,512]{2,1,0:T(8,128)(2,1)}), bf16[64,32,512]{2,1,0:T(8,128)(2,1)S(1)}, u32[]{:S(2)}, u32[]{:S(2)}) async-start(bf16[64,32,512]{2,1,0:T(8,128)(2,1)} %broadcast_select_fusion), calls=%async_computation.2 | async-start | bytes 4194304 | tf_op jit(solution)/shard_map/all_to_all | solution.py:177
  436.8 347.9 %all-reduce.7.cloned.1.call-start = ((), (), s32[]{:S(2)}) async-start(), calls=%async_computation.4 | async-start | bytes 8388608 | tf_op jit(solution)/shard_map/psum | solution.py:180
  629.5 0.7 copy-start.6
  784.7 4.0 copy-start.4
  784.7 5.0 copy-start.1
Sparse Core Ops, SparseCore 0:
  413.9 215.5 all-reduce.4
  632.0 96.7 all-reduce.6
